TPU v7x, 32 devices: a whole 2x2x4 slice. The times are simulated.
32 devices in a mesh: dp: 8 (over y, x, core), tensor: 4 (over z).
Axes of the slice: x: 2, y: 2, z: 4, core: 2. Of those that a mesh axis runs over, the one named last changes fastest.
Arguments:
- activations: bfloat16 [8, 2048, 2048], P('dp', 'tensor'), may hold values from -6 to 6
- segment_ids: int32 [8, 2048], P('dp'), may hold values from 0 to 3, as said below
- attn_gain: float32 [2048], replicated, may hold values from 0.1 to 1.9
- w_query: bfloat16 [2048, 2048], P('dp', 'tensor'), may hold values from -0.125 to 0.125
- w_key: bfloat16 [2048, 512], P('dp', 'tensor'), may hold values from -0.125 to 0.125
- w_value: bfloat16 [2048, 512], P('dp', 'tensor'), may hold values from -0.125 to 0.125
- w_out: bfloat16 [2048, 2048], P('dp', 'tensor'), may hold values from -0.375 to 0.375
- mlp_gain: float32 [2048], replicated, may hold values from 0.1 to 1.9
- w_gate: bfloat16 [2048, 8192], P('dp', 'tensor'), may hold values from -0.125 to 0.125
- w_up: bfloat16 [2048, 8192], P('dp', 'tensor'), may hold values from -0.125 to 0.125
- w_down: bfloat16 [2048, 8192], P('dp', 'tensor'), may hold values from -0.09375 to 0.09375
- cotangent: bfloat16 [8, 2048, 2048], P('dp', 'tensor'), may hold values from -6 to 6
Outputs:
- output: bfloat16 [8, 2048, 2048], P('dp', 'tensor')
- input_grad: bfloat16 [8, 2048, 2048], P('dp', 'tensor')
- attn_gain_grad: float32 [2048], replicated
- w_query_grad: float32 [2048, 2048], P('dp', 'tensor')
- w_key_grad: float32 [2048, 512], P('dp', 'tensor')
- w_value_grad: float32 [2048, 512], P('dp', 'tensor')
- w_out_grad: float32 [2048, 2048], P('dp', 'tensor')
- mlp_gain_grad: float32 [2048], replicated
- w_gate_grad: float32 [2048, 8192], P('dp', 'tensor')
- w_up_grad: float32 [2048, 8192], P('dp', 'tensor')
- w_down_grad: float32 [2048, 8192], P('dp', 'tensor')
Inputs may be any that keep to these rules, and one draw needn't show every extreme that they name: `segment_ids`: along each sequence the ids never fall; each of the 4 documents has 204 to 1024 tokens, and exactly one document of each sequence has 1024.
All inputs are finite; a program needn't handle non-finite values.
Results may differ from a plain program's by a relative error of at most 0.018.
Values may be sent and summed in bfloat16 or wider, within the bound.
A program may use at most 320 MiB of HBM per device.

v0:
```python
import math
import jax
import jax.numpy as jnp
from jax import lax
from jax.sharding import PartitionSpec as P

HEAD_DIM = 64
DOCS = 4
QBLOCK = 512
NORM_EPS = 1e-05
ROPE_THETA = 500000.0


def matmul(left, right):
    return jnp.dot(left, right, preferred_element_type=jnp.float32)


def matmul_nt(left, right):
    return lax.dot_general(
        left, right, (((1,), (1,)), ((), ())), preferred_element_type=jnp.float32
    )


def matmul_tn(left, right):
    return lax.dot_general(
        left, right, (((0,), (0,)), ((), ())), preferred_element_type=jnp.float32
    )


def rope_tables(segments):
    length = segments.shape[-1]
    doc_ids = jnp.arange(DOCS, dtype=jnp.int32)
    member = (segments[..., :, None] == doc_ids).astype(jnp.int32)
    counts = jnp.sum(member, axis=-2)
    before = (doc_ids < segments[..., :, None]).astype(jnp.int32)
    first = jnp.sum(before * counts[..., None, :], axis=-1)
    position = (jnp.arange(length, dtype=jnp.int32) - first).astype(jnp.float32)
    frequency = jnp.exp(
        jnp.arange(HEAD_DIM // 2, dtype=jnp.float32) * (-2.0 * math.log(ROPE_THETA) / HEAD_DIM)
    )
    angles = position[..., None] * frequency
    return (jnp.cos(angles), jnp.sin(angles))


def rotate(values_in, cosine, sine_tab):
    half_dim = HEAD_DIM // 2
    first_half = values_in[..., :half_dim]
    second_half = values_in[..., half_dim:]
    cos_wide = cosine[..., None, :]
    sin_wide = sine_tab[..., None, :]
    return jnp.concatenate(
        [
            first_half * cos_wide - second_half * sin_wide,
            second_half * cos_wide + first_half * sin_wide,
        ],
        axis=-1,
    )


def rotate_back(grad_in, cosine, sine_tab):
    half_dim = HEAD_DIM // 2
    first_half = grad_in[..., :half_dim]
    second_half = grad_in[..., half_dim:]
    cos_wide = cosine[..., None, :]
    sin_wide = sine_tab[..., None, :]
    return jnp.concatenate(
        [
            first_half * cos_wide + second_half * sin_wide,
            second_half * cos_wide - first_half * sin_wide,
        ],
        axis=-1,
    )


def rms_scale(values_in):
    return lax.rsqrt(jnp.mean(values_in * values_in, axis=-1, keepdims=True) + NORM_EPS)


def norm_back(values_in, scaling, gain, grad_in):
    gained = grad_in * gain
    gain_part = jnp.sum(grad_in * values_in * scaling, axis=(0, 1))
    inner = jnp.mean(gained * values_in, axis=-1, keepdims=True)
    return (gain_part, scaling * gained - values_in * scaling * scaling * scaling * inner)


def gather_rows(local_rows):
    return lax.all_gather(local_rows, "tensor", axis=1, tiled=True)


def sum_rows(partial_rows):
    return lax.psum_scatter(partial_rows, "tensor", scatter_dimension=1, tiled=True)


def block_inputs(block_id, query_rot, key_rot, value_rows, segment_ids):
    length = segment_ids.shape[1]
    blocks = length // QBLOCK
    seq_id = block_id // blocks
    offset = block_id % blocks * QBLOCK
    query_seq = lax.dynamic_index_in_dim(query_rot, seq_id, 0, False)
    query_block = lax.dynamic_slice_in_dim(query_seq, offset, QBLOCK, 0)
    key_seq = lax.dynamic_index_in_dim(key_rot, seq_id, 0, False)
    value_seq = lax.dynamic_index_in_dim(value_rows, seq_id, 0, False)
    seg_seq = lax.dynamic_index_in_dim(segment_ids, seq_id, 0, False)
    query_seg = lax.dynamic_slice_in_dim(seg_seq, offset, QBLOCK, 0)
    query_pos = offset + jnp.arange(QBLOCK, dtype=jnp.int32)
    key_pos = jnp.arange(length, dtype=jnp.int32)
    allowed = (query_seg[:, None] == seg_seq[None, :]) & (key_pos[None, :] <= query_pos[:, None])
    score = jnp.einsum(
        "qkgd,skd->kgqs", query_block, key_seq, preferred_element_type=jnp.float32
    ) * HEAD_DIM ** (-0.5)
    score = jnp.where(allowed, score, -1e30)
    return (seq_id, offset, query_block, key_seq, value_seq, score)


def attend(query_rot, key_rot, value_rows, segment_ids):
    seq_count, length = segment_ids.shape

    def one_block(block_id):
        seq_id, offset, query_block, key_seq, value_seq, score = block_inputs(
            block_id, query_rot, key_rot, value_rows, segment_ids
        )
        row_max = jnp.max(score, axis=-1, keepdims=True)
        expd = jnp.exp(score - row_max)
        row_sum = jnp.sum(expd, axis=-1, keepdims=True)
        weights = (expd / row_sum).astype(jnp.bfloat16)
        result = jnp.einsum(
            "kgqs,skd->qkgd", weights, value_seq, preferred_element_type=jnp.float32
        ).astype(jnp.bfloat16)
        return (result, row_max[..., 0] + jnp.log(row_sum[..., 0]))

    count_blocks = seq_count * (length // QBLOCK)
    results, log_sums = lax.map(one_block, jnp.arange(count_blocks, dtype=jnp.int32))
    return (results.reshape(seq_count, length, *results.shape[2:]), log_sums)


def attend_back(query_rot, key_rot, value_rows, grad_att, log_sums, segment_ids):
    seq_count, length = segment_ids.shape
    blocks = length // QBLOCK

    def one_block(block_id):
        seq_id, offset, query_block, key_seq, value_seq, score = block_inputs(
            block_id, query_rot, key_rot, value_rows, segment_ids
        )
        grad_seq = lax.dynamic_index_in_dim(grad_att, seq_id, 0, False)
        grad_block = lax.dynamic_slice_in_dim(grad_seq, offset, QBLOCK, 0)
        lse_block = lax.dynamic_index_in_dim(log_sums, block_id, 0, False)
        prob_rows = jnp.exp(score - lse_block[..., None])
        weights = prob_rows.astype(jnp.bfloat16)
        grad_weights = jnp.einsum(
            "qkgd,skd->kgqs", grad_block, value_seq, preferred_element_type=jnp.float32
        )
        row_dot = jnp.sum(grad_weights * prob_rows, axis=-1, keepdims=True)
        grad_score = (prob_rows * (grad_weights - row_dot)).astype(jnp.bfloat16)
        scaling = HEAD_DIM ** (-0.5)
        grad_query = (
            jnp.einsum("kgqs,skd->qkgd", grad_score, key_seq, preferred_element_type=jnp.float32)
            * scaling
        )
        grad_key = (
            jnp.einsum(
                "kgqs,qkgd->skd", grad_score, query_block, preferred_element_type=jnp.float32
            )
            * scaling
        )
        grad_value = jnp.einsum(
            "kgqs,qkgd->skd", weights, grad_block, preferred_element_type=jnp.float32
        )
        return (grad_query, grad_key, grad_value)

    grad_query, grad_key, grad_value = lax.map(
        one_block, jnp.arange(seq_count * blocks, dtype=jnp.int32)
    )
    grad_query = grad_query.reshape(seq_count, length, *grad_query.shape[2:])
    grad_key = jnp.sum(grad_key.reshape(seq_count, blocks, length, *grad_key.shape[2:]), axis=1)
    grad_value = jnp.sum(
        grad_value.reshape(seq_count, blocks, length, *grad_value.shape[2:]), axis=1
    )
    return (grad_query, grad_key, grad_value)


def per_device(
    activations,
    segment_ids,
    attn_gain,
    w_query,
    w_key,
    w_value,
    w_out,
    mlp_gain,
    w_gate,
    w_up,
    w_down,
    cotangent,
):
    seq_count, row_count, model_width = activations.shape
    length = segment_ids.shape[1]
    tok_count = seq_count * length
    kv_local = w_key.shape[1] // HEAD_DIM
    head_local = w_query.shape[1] // HEAD_DIM
    group_size = head_local // kv_local
    cosine, sine_tab = rope_tables(segment_ids)
    attn_full = (
        lax.all_gather(w_query, "dp", axis=0, tiled=True),
        lax.all_gather(w_key, "dp", axis=0, tiled=True),
        lax.all_gather(w_value, "dp", axis=0, tiled=True),
        lax.all_gather(w_out, "dp", axis=0, tiled=True),
    )
    x_float = activations.astype(jnp.float32)
    scale_one = rms_scale(x_float)
    normed = gather_rows((x_float * scale_one * attn_gain).astype(jnp.bfloat16)).reshape(
        tok_count, model_width
    )
    query_rot = rotate(
        matmul(normed, attn_full[0]).reshape(seq_count, length, head_local, HEAD_DIM),
        cosine,
        sine_tab,
    )
    query_rot = query_rot.astype(jnp.bfloat16).reshape(
        seq_count, length, kv_local, group_size, HEAD_DIM
    )
    key_rot = rotate(
        matmul(normed, attn_full[1]).reshape(seq_count, length, kv_local, HEAD_DIM),
        cosine,
        sine_tab,
    ).astype(jnp.bfloat16)
    value_rows = (
        matmul(normed, attn_full[2])
        .astype(jnp.bfloat16)
        .reshape(seq_count, length, kv_local, HEAD_DIM)
    )
    attended, log_sums = attend(query_rot, key_rot, value_rows, segment_ids)
    attended_flat = attended.reshape(tok_count, head_local * HEAD_DIM)
    resid = x_float + sum_rows(
        matmul_nt(attended_flat, attn_full[3]).reshape(seq_count, length, model_width)
    )
    mlp_full = (
        lax.all_gather(w_gate, "dp", axis=0, tiled=True),
        lax.all_gather(w_up, "dp", axis=0, tiled=True),
        lax.all_gather(w_down, "dp", axis=0, tiled=True),
    )
    scale_two = rms_scale(resid)
    normed_mlp = gather_rows((resid * scale_two * mlp_gain).astype(jnp.bfloat16)).reshape(
        tok_count, model_width
    )
    gate_pre = matmul(normed_mlp, mlp_full[0])
    up_proj = matmul(normed_mlp, mlp_full[1])
    hidden = (jax.nn.silu(gate_pre) * up_proj).astype(jnp.bfloat16)
    output = (
        resid + sum_rows(matmul_nt(hidden, mlp_full[2]).reshape(seq_count, length, model_width))
    ).astype(jnp.bfloat16)
    mlp_back = (
        lax.all_gather(w_gate, "dp", axis=0, tiled=True),
        lax.all_gather(w_up, "dp", axis=0, tiled=True),
        lax.all_gather(w_down, "dp", axis=0, tiled=True),
    )
    grad_full = gather_rows(cotangent).reshape(tok_count, model_width)
    grad_down_w = matmul_tn(grad_full, hidden)
    grad_hidden = matmul(grad_full, mlp_back[2])
    sigma = jax.nn.sigmoid(gate_pre)
    grad_gate = (grad_hidden * up_proj * sigma * (1.0 + gate_pre * (1.0 - sigma))).astype(
        jnp.bfloat16
    )
    grad_up = (grad_hidden * gate_pre * sigma).astype(jnp.bfloat16)
    grad_gate_w = matmul_tn(normed_mlp, grad_gate)
    grad_up_w = matmul_tn(normed_mlp, grad_up)
    grad_normed_mlp = matmul_nt(grad_gate, mlp_back[0]) + matmul_nt(grad_up, mlp_back[1])
    grad_normed_mlp = sum_rows(grad_normed_mlp.reshape(seq_count, length, model_width))
    gain_two_part, grad_resid_norm = norm_back(resid, scale_two, mlp_gain, grad_normed_mlp)
    grad_resid = cotangent.astype(jnp.float32) + grad_resid_norm
    attn_back = (
        lax.all_gather(w_query, "dp", axis=0, tiled=True),
        lax.all_gather(w_key, "dp", axis=0, tiled=True),
        lax.all_gather(w_value, "dp", axis=0, tiled=True),
        lax.all_gather(w_out, "dp", axis=0, tiled=True),
    )
    grad_resid_full = gather_rows(grad_resid.astype(jnp.bfloat16)).reshape(tok_count, model_width)
    grad_out_w = matmul_tn(grad_resid_full, attended_flat)
    grad_att = matmul(grad_resid_full, attn_back[3]).astype(jnp.bfloat16)
    grad_att = grad_att.reshape(seq_count, length, kv_local, group_size, HEAD_DIM)
    grad_query_rot, grad_key_rot, grad_value_rows = attend_back(
        query_rot, key_rot, value_rows, grad_att, log_sums, segment_ids
    )
    grad_query = rotate_back(
        grad_query_rot.reshape(seq_count, length, head_local, HEAD_DIM), cosine, sine_tab
    )
    grad_query = grad_query.astype(jnp.bfloat16).reshape(tok_count, head_local * HEAD_DIM)
    grad_key = (
        rotate_back(grad_key_rot, cosine, sine_tab)
        .astype(jnp.bfloat16)
        .reshape(tok_count, kv_local * HEAD_DIM)
    )
    grad_value = grad_value_rows.astype(jnp.bfloat16).reshape(tok_count, kv_local * HEAD_DIM)
    grad_query_w = matmul_tn(normed, grad_query)
    grad_key_w = matmul_tn(normed, grad_key)
    grad_value_w = matmul_tn(normed, grad_value)
    grad_normed = (
        matmul_nt(grad_query, attn_back[0])
        + matmul_nt(grad_key, attn_back[1])
        + matmul_nt(grad_value, attn_back[2])
    )
    grad_normed = sum_rows(grad_normed.reshape(seq_count, length, model_width))
    gain_one_part, grad_x_norm = norm_back(x_float, scale_one, attn_gain, grad_normed)
    input_grad = (grad_resid + grad_x_norm).astype(jnp.bfloat16)
    gain_totals = lax.psum((gain_one_part, gain_two_part), ("dp", "tensor"))
    all_sums = (
        lax.psum_scatter(
            grad_query_w.astype(jnp.bfloat16), "dp", scatter_dimension=0, tiled=True
        ).astype(jnp.float32),
        lax.psum_scatter(
            grad_key_w.astype(jnp.bfloat16), "dp", scatter_dimension=0, tiled=True
        ).astype(jnp.float32),
        lax.psum_scatter(
            grad_value_w.astype(jnp.bfloat16), "dp", scatter_dimension=0, tiled=True
        ).astype(jnp.float32),
        lax.psum_scatter(
            grad_out_w.astype(jnp.bfloat16), "dp", scatter_dimension=0, tiled=True
        ).astype(jnp.float32),
        lax.psum_scatter(
            grad_gate_w.astype(jnp.bfloat16), "dp", scatter_dimension=0, tiled=True
        ).astype(jnp.float32),
        lax.psum_scatter(
            grad_up_w.astype(jnp.bfloat16), "dp", scatter_dimension=0, tiled=True
        ).astype(jnp.float32),
        lax.psum_scatter(
            grad_down_w.astype(jnp.bfloat16), "dp", scatter_dimension=0, tiled=True
        ).astype(jnp.float32),
    )
    attn_sums = all_sums[:4]
    mlp_sums = all_sums[4:]
    return (
        output,
        input_grad,
        gain_totals[0],
        attn_sums[0],
        attn_sums[1],
        attn_sums[2],
        attn_sums[3],
        gain_totals[1],
        mlp_sums[0],
        mlp_sums[1],
        mlp_sums[2],
    )


def solution(mesh):
    in_specs = (
        P("dp", "tensor", None),
        P("dp", None),
        P(),
        P("dp", "tensor"),
        P("dp", "tensor"),
        P("dp", "tensor"),
        P("dp", "tensor"),
        P(),
        P("dp", "tensor"),
        P("dp", "tensor"),
        P("dp", "tensor"),
        P("dp", "tensor", None),
    )
    out_specs = (
        P("dp", "tensor", None),
        P("dp", "tensor", None),
        P(),
        P("dp", "tensor"),
        P("dp", "tensor"),
        P("dp", "tensor"),
        P("dp", "tensor"),
        P(),
        P("dp", "tensor"),
        P("dp", "tensor"),
        P("dp", "tensor"),
    )
    return jax.shard_map(
        per_device, mesh=mesh, in_specs=in_specs, out_specs=out_specs, check_vma=False
    )
```

profile of v0, /device:TPU:0, one launch (start us, length us, event | category | flops | bytes accessed | tf_op | source)
XLA Modules:
  0.0 2988.1 jit_solution(1791326415638827385)
XLA Ops:
  45.6 149.2 %all-gather.10.cloned.1.call-done = bf16[1,2048,2048]{2,1,0:T(8,128)(2,1)} async-done(((bf16[1,512,2048]{2,1,0:T(8,128)(2,1)}), bf16[1,2048,2048]{2,1,0:T(8,128)(2,1)}) %all-gather.10.cloned.1.call-update) | async-done | bytes 8388624 | tf_op jit(solution)/shard_map/all_gather | solution.py:87
  211.1 199.4 %while.30 = (s32[]{:T(128)}, bf16[4,512,2,4,64]{1,4,3,2,0:T(8,128)(2,1)}, f32[4,2,4,512]{3,2,1,0:T(4,128)}, s32[4]{0:T(128)S(1)}, s32[1,2048]{1,0:T(1,128)S(1)},...) while((s32[]{:T(128)}, ...), condition=%wide.region_6.7_spmd, body=%wide.region_3.6_spmd.sunk | while | flops 2251551232 | bytes 107104584 | solution.py:132
  429.4 278.2 %reduce-scatter.12.cloned.1.call-done = f32[1,512,2048]{2,1,0:T(8,128)} async-done(((f32[1,2048,2048]{2,1,0:T(8,128)}), f32[1,512,2048]{2,1,0:T(8,128)}) %reduce-scatter.12.cloned.1.call-update) | async-done | bytes 4194320 | tf_op jit(solution)/shard_map/reduce_scatter | solution.py:91
  716.5 48.2 %all-gather.20.cloned.1.call-done = bf16[2048,2048]{1,0:T(8,128)(2,1)} async-done(((bf16[256,2048]{1,0:T(8,128)(2,1)}), bf16[2048,2048]{1,0:T(8,128)(2,1)}) %all-gather.20.cloned.1.call-update) | async-done | bytes 8388624 | tf_op jit(solution)/shard_map/all_gather | solution.py:238
  764.6 151.7 %all-gather.16.cloned.1.call-done = bf16[1,2048,2048]{2,1,0:T(8,128)(2,1)} async-done(((bf16[1,512,2048]{2,1,0:T(8,128)(2,1)}), bf16[1,2048,2048]{2,1,0:T(8,128)(2,1)}) %all-gather.16.cloned.1.call-update) | async-done | bytes 8388624 | tf_op jit(solution)/shard_map/all_gather | solution.py:87
  940.7 30.3 %all-gather.18.cloned.1.call-done = bf16[2048,2048]{1,0:T(8,128)(2,1)} async-done(((bf16[256,2048]{1,0:T(8,128)(2,1)}), bf16[2048,2048]{1,0:T(8,128)(2,1)}) %all-gather.18.cloned.1.call-update) | async-done | bytes 8388624 | tf_op jit(solution)/shard_map/all_gather | solution.py:237
  995.3 127.1 %all-gather.24.cloned.1.call-done = bf16[1,2048,2048]{2,1,0:T(8,128)(2,1)} async-done(((bf16[1,512,2048]{2,1,0:T(8,128)(2,1)}), bf16[1,2048,2048]{2,1,0:T(8,128)(2,1)}) %all-gather.24.cloned.1.call-update) | async-done | bytes 8388624 | tf_op jit(solution)/shard_map/all_gather | solution.py:87
  1122.4 54.7 %all-gather.22.cloned.1.call-done = bf16[2048,2048]{1,0:T(8,128)(2,1)} async-done(((bf16[256,2048]{1,0:T(8,128)(2,1)}), bf16[2048,2048]{1,0:T(8,128)(2,1)}) %all-gather.22.cloned.1.call-update) | async-done | bytes 8388624 | tf_op jit(solution)/shard_map/all_gather | solution.py:239
  1177.1 34.8 %multiply_convert_fusion = (bf16[2048,2048]{1,0:T(8,128)(2,1)}, bf16[2048,2048]{1,0:T(8,128)(2,1)}, bf16[2048,2048]{1,0:T(8,128)(2,1)}) fusion(f32[2048,2048]{1,0:T(8,128)} %fusion.67, f32[2048,2048]{1,0:T(8,128)} %fusion.65, bf16[2048,2048]{1,0:T(8,128)(2,1)} %all-gather.22.cloned.1.call-done, bf16[1,2048,2048]{2,1,0:T(8,128)(2,1)} %all-gather.24.cloned.1.call-done), kind=kOutput, calls=%fused_computation.67 | convolution fusion | flops 17246978048 | bytes 75497472 | tf_op jit(solution)/shard_map/dot_general | solution.py:15
  1236.2 26.7 add_bitcast_fusion.1
  1263.0 280.4 %reduce-scatter.16.cloned.1.call-done = f32[1,512,2048]{2,1,0:T(8,128)} async-done(((f32[1,2048,2048]{2,1,0:T(8,128)}), f32[1,512,2048]{2,1,0:T(8,128)}) %reduce-scatter.16.cloned.1.call-update) | async-done | bytes 4194320 | tf_op jit(solution)/shard_map/reduce_scatter | solution.py:91
  1624.0 78.7 %all-gather.26.cloned.1.call-done = bf16[1,2048,2048]{2,1,0:T(8,128)(2,1)} async-done(((bf16[1,512,2048]{2,1,0:T(8,128)(2,1)}), bf16[1,2048,2048]{2,1,0:T(8,128)(2,1)}) %all-gather.26.cloned.1.call-update) | async-done | bytes 8388624 | tf_op jit(solution)/shard_map/all_gather | solution.py:87
  1712.6 521.1 %while.31 = (s32[]{:T(128)}, f32[4,512,2,4,64]{1,0,4,3,2:T(4,128)}, f32[4,2048,2,64]{1,3,2,0:T(8,128)}, f32[4,2048,2,64]{1,3,2,0:T(8,128)}, s32[4]{0:T(128)S(1)}...) while((s32[]{:T(128)}, f32[4,512,2,4,64]{1,0,4,3,2:T(4,128)}, ...), condition=%wide.region_14.15_spmd, body=%wide.region_12.14_spmd.sunk | while | flops 5498204672 | bytes 367659456 | solution.py:170
  1750.0 26.5 fusion.192
  1776.5 31.1 %fusion.193 = bf16[2,4,512,2048]{3,2,1,0:T(8,128)(2,1)} fusion(f32[2,512,4,2048]{3,1,2,0:T(8,128)} %get-tuple-element.479, f32[2,512,4,2048]{3,1,2,0:T(8,128)} %fusion.190, f32[2,4,512]{2,1,0:T(4,128)S(1)} %get-tuple-element.480, f32[2,4,512]{2,1,0:T(4,128)S(1)} %dynamic-slice_bitcast_fusion.2, pred[512,2048]{1,0:T(8,128)(4,1)S(1)} %fusion.191), kind=kLoop, calls=%fused_computation.27.clone.1 | loop fusion | flops 50331648 | bytes 84967424 | tf_op jit(solution)/shard_map/while/body/eval_jaxpr/convert_element_type | solution.py:153
  1886.3 26.4 fusion.192
  1912.8 28.3 fusion.193
  2014.3 26.3 fusion.192
  2040.6 27.7 fusion.193
  2167.8 27.7 fusion.193
  2360.8 43.2 %reduce-scatter.20.cloned.1.call-done = bf16[256,512]{1,0:T(8,128)(2,1)} async-done(((bf16[2048,512]{1,0:T(8,128)(2,1)}), bf16[256,512]{1,0:T(8,128)(2,1)}) %reduce-scatter.20.cloned.1.call-update) | async-done | bytes 262160 | tf_op jit(solution)/shard_map/reduce_scatter | solution.py:306
  2405.8 281.0 %reduce-scatter.18.cloned.1.call-done = f32[1,512,2048]{2,1,0:T(8,128)} async-done(((f32[1,2048,2048]{2,1,0:T(8,128)}), f32[1,512,2048]{2,1,0:T(8,128)}) %reduce-scatter.18.cloned.1.call-update) | async-done | bytes 4194320 | tf_op jit(solution)/shard_map/reduce_scatter | solution.py:91
  2690.3 46.1 %all-reduce = (f32[2048]{0:T(1024)}, f32[2048]{0:T(1024)}) all-reduce(f32[2048]{0:T(1024)S(1)} %get-tuple-element.294, f32[2048]{0:T(1024)S(1)} %copy-done.38), channel_id=1, replica_groups=mesh['dp'=8,'tensor'=4] {'dp','tensor'}, use_global_device_ids=true, to_apply=%region_20.21 | all-reduce | flops 4096 | bytes 32768 | tf_op jit(solution)/shard_map/psum | solution.py:304
  2736.4 234.7 %reduce-scatter.14.cloned.1.call-done = f32[1,512,2048]{2,1,0:T(8,128)} async-done(((f32[1,2048,2048]{2,1,0:T(8,128)}), f32[1,512,2048]{2,1,0:T(8,128)}) %reduce-scatter.14.cloned.1.call-update) | async-done | bytes 4194320 | tf_op jit(solution)/shard_map/reduce_scatter | solution.py:91
  (292 shorter events, 891.2 us)
Async XLA Ops:
  7.2 35.5 %all-gather.12.cloned.1.call-start = ((), (), s32[]{:S(2)}) async-start(), calls=%async_computation.12 | async-start | bytes 2359296 | tf_op jit(solution)/shard_map/all_gather | solution.py:203
  7.9 186.9 %all-gather.10.cloned.1.call-start = ((), (), s32[]{:S(2)}) async-start(), calls=%async_computation.11 | async-start | bytes 10485760 | tf_op jit(solution)/shard_map/all_gather | solution.py:87
  13.6 402.6 %all-gather.14.cloned.1.call-start = ((), (), s32[]{:S(2)}) async-start(), calls=%async_computation.13 | async-start | bytes 2359296 | tf_op jit(solution)/shard_map/all_gather | solution.py:206
  14.3 693.3 %reduce-scatter.12.cloned.1.call-start = ((), (), s32[]{:S(2)}) async-start(), calls=%async_computation.14 | async-start | bytes 20971520 | tf_op jit(solution)/shard_map/reduce_scatter | solution.py:91
  428.7 335.9 %all-gather.20.cloned.1.call-start = ((), (), s32[]{:S(2)}) async-start(), calls=%async_computation.17 | async-start | bytes 9437184 | tf_op jit(solution)/shard_map/all_gather | solution.py:238
  429.3 487.0 %all-gather.16.cloned.1.call-start = ((), (), s32[]{:S(2)}) async-start(), calls=%async_computation.15 | async-start | bytes 10485760 | tf_op jit(solution)/shard_map/all_gather | solution.py:87
  714.2 256.9 %all-gather.18.cloned.1.call-start = ((), (), s32[]{:S(2)}) async-start(), calls=%async_computation.16 | async-start | bytes 9437184 | tf_op jit(solution)/shard_map/all_gather | solution.py:237
  714.9 407.5 %all-gather.24.cloned.1.call-start = ((), (), s32[]{:S(2)}) async-start(), calls=%async_computation.20 | async-start | bytes 10485760 | tf_op jit(solution)/shard_map/all_gather | solution.py:87
  715.7 461.4 %all-gather.22.cloned.1.call-start = ((), (), s32[]{:S(2)}) async-start(), calls=%async_computation.18 | async-start | bytes 9437184 | tf_op jit(solution)/shard_map/all_gather | solution.py:239
  716.4 827.0 %reduce-scatter.16.cloned.1.call-start = ((), (), s32[]{:S(2)}) async-start(), calls=%async_computation.21 | async-start | bytes 20971520 | tf_op jit(solution)/shard_map/reduce_scatter | solution.py:91
  1262.9 439.8 %all-gather.26.cloned.1.call-start = ((), (), s32[]{:S(2)}) async-start(), calls=%async_computation.22 | async-start | bytes 10485760 | tf_op jit(solution)/shard_map/all_gather | solution.py:87
  1552.2 790.1 %reduce-scatter.32.cloned.1.call-start = ((), (), s32[]{:S(2)}) async-start(), calls=%async_computation.30 | async-start | bytes 9437184 | tf_op jit(solution)/shard_map/reduce_scatter | solution.py:324
  1576.0 768.8 %reduce-scatter.30.cloned.1.call-start = ((), (), s32[]{:S(2)}) async-start(), calls=%async_computation.29 | async-start | bytes 9437184 | tf_op jit(solution)/shard_map/reduce_scatter | solution.py:321
  1600.0 747.8 %reduce-scatter.28.cloned.1.call-start = ((), (), s32[]{:S(2)}) async-start(), calls=%async_computation.28 | async-start | bytes 9437184 | tf_op jit(solution)/shard_map/reduce_scatter | solution.py:318
  1624.0 726.7 %reduce-scatter.22.cloned.1.call-start = ((), (), s32[]{:S(2)}) async-start(), calls=%async_computation.25 | async-start | bytes 589824 | tf_op jit(solution)/shard_map/reduce_scatter | solution.py:309
  2243.2 108.9 %reduce-scatter.24.cloned.1.call-start = ((), (), s32[]{:S(2)}) async-start(), calls=%async_computation.26 | async-start | bytes 589824 | tf_op jit(solution)/shard_map/reduce_scatter | solution.py:312
  2252.6 106.5 %reduce-scatter.26.cloned.1.call-start = ((), (), s32[]{:S(2)}) async-start(), calls=%async_computation.27 | async-start | bytes 2359296 | tf_op jit(solution)/shard_map/reduce_scatter | solution.py:315
  2262.6 141.4 %reduce-scatter.20.cloned.1.call-start = ((), (), s32[]{:S(2)}) async-start(), calls=%async_computation.24 | async-start | bytes 2359296 | tf_op jit(solution)/shard_map/reduce_scatter | solution.py:306
  2282.9 404.0 %reduce-scatter.18.cloned.1.call-start = ((), (), s32[]{:S(2)}) async-start(), calls=%async_computation.23 | async-start | bytes 20971520 | tf_op jit(solution)/shard_map/reduce_scatter | solution.py:91
  2317.5 653.5 %reduce-scatter.14.cloned.1.call-start = ((), (), s32[]{:S(2)}) async-start(), calls=%async_computation.19 | async-start | bytes 20971520 | tf_op jit(solution)/shard_map/reduce_scatter | solution.py:91
  2344.8 342.0 %copy-start.37 = (f32[512]{0:T(512)S(1)}, f32[512]{0:T(512)}, u32[]{:S(2)}) copy-start(f32[512]{0:T(512)} %copy-done.36) | copy-start | bytes 6148
  2350.6 620.5 %copy-start.29 = (f32[2048]{0:T(1024)S(1)}, f32[2048]{0:T(1024)}, u32[]{:S(2)}) copy-start(f32[2048]{0:T(1024)} %param.23) | copy-start | bytes 24580
  2350.6 620.5 %copy-start.35 = (f32[512]{0:T(512)S(1)}, f32[512]{0:T(512)}, u32[]{:S(2)}) copy-start(f32[512]{0:T(512)} %copy-done.33) | copy-start | bytes 6148
  2350.6 620.5 %copy-start.40 = (f32[512]{0:T(512)S(1)}, f32[512]{0:T(512)}, u32[]{:S(2)}) copy-start(f32[512]{0:T(512)} %copy-done.39) | copy-start | bytes 6148
  (46 other events, 3535.2 us)
Sparse Core Ops, SparseCore 0:
  9.9 32.7 all-gather.11
  44.8 149.9 all-gather.9
  196.7 26.1 all-gather.13
  428.8 278.6 reduce-scatter.11
  709.5 55.1 all-gather.19
  766.7 149.6 all-gather.15
  918.4 52.6 all-gather.17
  972.7 149.6 all-gather.23
  1124.4 52.6 all-gather.21
  1263.1 280.2 reduce-scatter.15
  1552.3 150.3 all-gather.25
  1706.0 69.5 reduce-scatter.31
  1779.5 71.2 reduce-scatter.29
  1854.1 71.2 reduce-scatter.27
  2243.4 32.6 reduce-scatter.21
  2279.6 34.1 reduce-scatter.23
  2317.8 41.2 reduce-scatter.25
  2362.8 41.2 reduce-scatter.19
  2406.5 280.2 reduce-scatter.17
  2689.0 282.0 reduce-scatter.13
where the time goes:
time: 3000 us; the launch traced here: 2990 us
  waiting for transfers between devices  1770 us (59%)
  matrix products  749 us (25%)
  other arithmetic  242 us (8%)
  local copies, waits for them, and re-layouts  119 us (4%)
  blocking collectives  69.5 us (2%)
    reduce_scatter x4, waiting for transfers between devices, sum_rows(): lax.psum_scatter(partial_rows, 'tensor', scatter_dimension=1, tiled=True)  1070 us
    all_gather x4, waiting for transfers between devices, gather_rows(): return lax.all_gather(local_rows, 'tensor', axis=1, tiled=True)  507 us
    dot_general x7, matrix products, matmul_nt(): lax.dot_general(left, right, (((1,), (1,)), ((), ())), preferred_element_...  123 us
    dot_general x8, matrix products, block_inputs(): jnp.einsum('qkgd,skd->kgqs', query_block, key_seq, preferred_element_type...  120 us
    convert_element_type x4, other arithmetic, one_block(): grad_score = (prob_rows * (grad_weights - row_dot)).astype(jnp.bfloat16)  115 us
    dot_general x7, matrix products, matmul(): return jnp.dot(left, right, preferred_element_type=jnp.float32)  107 us
    dot_general x4, matrix products, one_block(): jnp.einsum('qkgd,skd->kgqs', grad_block, value_seq, preferred_element_typ...  105 us
    dot_general x7, matrix products, matmul_tn(): lax.dot_general(left, right, (((0,), (0,)), ((), ())), preferred_element_...  104 us
  transfers between devices with their start and end apart: 20, of which 14 were waited for; matrix products, arithmetic and copies ran while one was open for 33% of the time, Pallas kernels for 0%

commit v1 on v0

--- a/solution.py
+++ b/solution.py
@@ -84,7 +84,35 @@
 
 
 def gather_rows(local_rows):
-    return lax.all_gather(local_rows, "tensor", axis=1, tiled=True)
+
+    def post_vector(mine):
+        named_axis = "tensor"
+        world_n = lax.axis_size(named_axis)
+        steps_seen = []
+        s = 0
+        while s < world_n:
+            steps_seen.append((s, (s + 1) % world_n))
+            s += 1
+        copies = []
+        s = 0
+        while s < world_n:
+            copies.append((s, (s - 1) % world_n))
+            s += 1
+        latest, vec_out = ([mine], [mine])
+        for _ in range(world_n // 2):
+            left_arr = lax.ppermute(latest[-1], named_axis, steps_seen)
+            latest.append(left_arr)
+        i0 = 0
+        while i0 < (world_n - 1) // 2:
+            w1 = lax.ppermute(vec_out[-1], named_axis, copies)
+            vec_out.append(w1)
+            i0 = i0 + 1
+        aux = jnp.concatenate([*latest[::-1], *vec_out[1:]], 1)
+        f_now = lax.axis_index(named_axis)
+        mat_out = jnp.roll(aux, (f_now - world_n // 2) * mine.shape[1], 1)
+        return mat_out
+
+    return post_vector(local_rows)
 
 
 def sum_rows(partial_rows):

time: 3000 us -> 2890 us (0.963)
  waiting for transfers between devices: 1770 us -> 1430 us
  other arithmetic: 242 us -> 391 us
  starting transfers between devices: 0.81 us -> 104 us
    all_gather x4 -> x0, waiting for transfers between devices: 507 us -> none  [gather_rows(): return lax.all_gather(local_rows, 'tensor', axis=1, tiled=True)]
    ppermute x0 -> x12, waiting for transfers between devices: none -> 311 us  [the longest x8 294 us: post_vector(): left_arr = lax.ppermute(latest[-1], named_axis, steps_seen)]
    reshape x0 -> x3, other arithmetic: none -> 123 us  [the longest x1 50.4 us: per_device(): gather_rows((resid * scale_two * mlp_gain).astype(jnp.bfloat16))]
    ppermute x0 -> x12, starting transfers between devices: none -> 104 us  [the longest x8 90.6 us: post_vector(): left_arr = lax.ppermute(latest[-1], named_axis, steps_seen)]
    all_gather x1, waiting for transfers between devices: 54.7 us -> 0.01 us  [per_device(): lax.all_gather(w_down, 'dp', axis=0, tiled=True)]
    all_gather x1, waiting for transfers between devices: 48.2 us -> 0.02 us  [per_device(): lax.all_gather(w_up, 'dp', axis=0, tiled=True)]
    all_gather x1, waiting for transfers between devices: 30.3 us -> 0.01 us  [per_device(): lax.all_gather(w_gate, 'dp', axis=0, tiled=True)]
  transfers between devices with their start and end apart: 20 -> 28, of which waited for: 14 -> 15; matrix products, arithmetic and copies ran while one was open for 33% -> 39% of each run, Pallas kernels for 0% -> 0%
where the time goes in v1:
time: 2890 us; the launch traced here: 2880 us
  waiting for transfers between devices  1430 us (49%)
  matrix products  735 us (25%)
  other arithmetic  391 us (14%)
  local copies, waits for them, and re-layouts  117 us (4%)
  starting transfers between devices  104 us (4%)
  blocking collectives  66.5 us (2%)
    reduce_scatter x4, waiting for transfers between devices, sum_rows(): lax.psum_scatter(partial_rows, 'tensor', scatter_dimension=1, tiled=True)  1060 us
    ppermute x8, waiting for transfers between devices, post_vector(): left_arr = lax.ppermute(latest[-1], named_axis, steps_seen)  294 us
    dot_general x7, matrix products, matmul_nt(): lax.dot_general(left, right, (((1,), (1,)), ((), ())), preferred_element_...  123 us
    dot_general x8, matrix products, block_inputs(): jnp.einsum('qkgd,skd->kgqs', query_block, key_seq, preferred_element_type...  116 us
    convert_element_type x4, other arithmetic, one_block(): grad_score = (prob_rows * (grad_weights - row_dot)).astype(jnp.bfloat16)  111 us
    dot_general x4, matrix products, one_block(): jnp.einsum('qkgd,skd->kgqs', grad_block, value_seq, preferred_element_typ...  105 us
    dot_general x7, matrix products, matmul_tn(): lax.dot_general(left, right, (((0,), (0,)), ((), ())), preferred_element_...  105 us
    dot_general x7, matrix products, matmul(): return jnp.dot(left, right, preferred_element_type=jnp.float32)  99.3 us
  transfers between devices with their start and end apart: 28, of which 15 were waited for; matrix products, arithmetic and copies ran while one was open for 39% of the time, Pallas kernels for 0%

profile of v1, /device:TPU:0, one launch (start us, length us, event | category | flops | bytes accessed | tf_op | source)
XLA Modules:
  0.0 2879.1 jit_solution(8493994120178935438)
XLA Ops:
  17.4 46.5 %collective-permute-done = bf16[1,512,2048]{2,1,0:T(8,128)(2,1)} collective-permute-done((bf16[1,512,2048]{2,1,0:T(8,128)(2,1)S(1)}, bf16[1,512,2048]{2,1,0:T(8,128)(2,1)}, u32[]{:S(2)}, u32[]{:S(2)}) %collective-permute-start) | collective-permute-done | bytes 2097184 | tf_op jit(solution)/shard_map/ppermute | solution.py:103
  107.6 45.3 %collective-permute-done.1 = bf16[1,512,2048]{2,1,0:T(8,128)(2,1)} collective-permute-done((bf16[1,512,2048]{2,1,0:T(8,128)(2,1)}, bf16[1,512,2048]{2,1,0:T(8,128)(2,1)}, u32[]{:S(2)}, u32[]{:S(2)}) %collective-permute-start.1) | collective-permute-done | bytes 2097184 | tf_op jit(solution)/shard_map/ppermute | solution.py:103
  153.0 29.2 %fusion.80 = bf16[1,2048,2048]{2,1,0:T(8,128)(2,1)S(1)} fusion(s32[]{:T(128)S(6)} %select_n.93, bf16[1,512,2048]{2,1,0:T(8,128)(2,1)} %collective-permute-done.1, bf16[1,512,2048]{2,1,0:T(8,128)(2,1)} %collective-permute-done, bf16[1,512,2048]{2,1,0:T(8,128)(2,1)S(1)} %fusion.98, bf16[1,512,2048]{2,1,0:T(8,128)(2,1)} %collective-permute-done.2), kind=kLoop, calls=%fused_computation.132 | loop fusion | flops 67108864 | bytes 16777220 | tf_op jit(solution)/shard_map/jit(_roll_dynamic)/concatenate | solution.py:112
  194.9 199.3 %while.30 = (s32[]{:T(128)}, bf16[4,512,2,4,64]{1,4,3,2,0:T(8,128)(2,1)}, f32[4,2,4,512]{3,2,1,0:T(4,128)}, s32[4]{0:T(128)S(1)}, s32[1,2048]{1,0:T(1,128)S(1)},...) while((s32[]{:T(128)}, ...), condition=%wide.region_6.8_spmd, body=%wide.region_3.7_spmd.sunk | while | flops 2251551232 | bytes 107104584 | solution.py:160
  414.2 317.5 %reduce-scatter.12.cloned.1.call-done = f32[1,512,2048]{2,1,0:T(8,128)} async-done(((f32[1,2048,2048]{2,1,0:T(8,128)}), f32[1,512,2048]{2,1,0:T(8,128)}) %reduce-scatter.12.cloned.1.call-update) | async-done | bytes 4194320 | tf_op jit(solution)/shard_map/reduce_scatter | solution.py:119
  744.8 42.7 %collective-permute-done.3 = bf16[1,512,2048]{2,1,0:T(8,128)(2,1)S(1)} collective-permute-done((bf16[1,512,2048]{2,1,0:T(8,128)(2,1)S(1)}, bf16[1,512,2048]{2,1,0:T(8,128)(2,1)S(1)}, u32[]{:S(2)}, u32[]{:S(2)}) %collective-permute-start.3) | collective-permute-done | bytes 2097184 | tf_op jit(solution)/shard_map/ppermute | solution.py:103
  787.5 43.6 %collective-permute-start.4 = (bf16[1,512,2048]{2,1,0:T(8,128)(2,1)S(1)}, bf16[1,512,2048]{2,1,0:T(8,128)(2,1)S(1)}, u32[]{:S(2)}, u32[]{:S(2)}) collective-permute-start(bf16[1,512,2048]{2,1,0:T(8,128)(2,1)S(1)} %collective-permute-done.3), channel_id=1, source_target_pairs={{0,1},{1,2},{2,3},{3,0},{4,5},{5,6},{6,7},{7,4},{8,9},{9,10},{10,1... | collective-permute-start | bytes 6291464 | tf_op jit(solution)/shard_map/ppermute | solution.py:103
  832.3 45.2 %collective-permute-done.7 = bf16[1,512,2048]{2,1,0:T(8,128)(2,1)S(1)} collective-permute-done((bf16[1,512,2048]{2,1,0:T(8,128)(2,1)}, bf16[1,512,2048]{2,1,0:T(8,128)(2,1)S(1)}, u32[]{:S(2)}, u32[]{:S(2)}) %collective-permute-start.7) | collective-permute-done | bytes 2097184 | tf_op jit(solution)/shard_map/ppermute | solution.py:103
  877.4 44.3 %fusion.65 = bf16[2048,2048]{1,0:T(8,128)(2,1)} fusion(s32[]{:T(128)S(6)} %select_n.93, bf16[1,512,2048]{2,1,0:T(8,128)(2,1)S(1)} %collective-permute-done.7, bf16[1,512,2048]{2,1,0:T(8,128)(2,1)} %collective-permute-done.6, bf16[1,512,2048]{2,1,0:T(8,128)(2,1)S(1)} %copy-done.11, bf16[1,512,2048]{2,1,0:T(8,128)(2,1)S(1)} %collective-permute-done.8), kind=kLoop, calls=%fused_computation.117 | loop fusion | flops 67108864 | bytes 16777220 | tf_op jit(solution)/shard_map/reshape | solution.py:284
  921.7 44.8 %collective-permute-done.4 = bf16[1,512,2048]{2,1,0:T(8,128)(2,1)S(1)} collective-permute-done((bf16[1,512,2048]{2,1,0:T(8,128)(2,1)S(1)}, bf16[1,512,2048]{2,1,0:T(8,128)(2,1)S(1)}, u32[]{:S(2)}, u32[]{:S(2)}) %collective-permute-start.4) | collective-permute-done | bytes 2097184 | tf_op jit(solution)/shard_map/ppermute | solution.py:103
  966.5 50.4 %fusion.73 = bf16[2048,2048]{1,0:T(8,128)(2,1)} fusion(s32[]{:T(128)S(6)} %select_n.93, bf16[1,512,2048]{2,1,0:T(8,128)(2,1)S(1)} %collective-permute-done.4, bf16[1,512,2048]{2,1,0:T(8,128)(2,1)S(1)} %collective-permute-done.3, bf16[1,512,2048]{2,1,0:T(8,128)(2,1)S(1)} %multiply_convert_fusion.3, bf16[1,512,2048]{2,1,0:T(8,128)(2,1)S(1)} %collective-permute-done.5), kind=kLoop, calls=%fused_computation.125 | loop fusion | flops 67108864 | bytes 16777220 | tf_op jit(solution)/shard_map/reshape | solution.py:270
  1065.3 34.8 %multiply_convert_fusion = (bf16[2048,2048]{1,0:T(8,128)(2,1)}, bf16[2048,2048]{1,0:T(8,128)(2,1)}, bf16[2048,2048]{1,0:T(8,128)(2,1)}) fusion(f32[2048,2048]{1,0:T(8,128)} %fusion.127, f32[2048,2048]{1,0:T(8,128)} %fusion.128, bf16[2048,2048]{1,0:T(8,128)(2,1)} %fusion.65, bf16[2048,2048]{1,0:T(8,128)(2,1)} %all-gather.14.cloned.1.call-done), kind=kOutput, calls=%fused_computation.99 | convolution fusion | flops 17246978048 | bytes 75497472 | tf_op jit(solution)/shard_map/dot_general | solution.py:15
  1199.1 231.2 %reduce-scatter.16.cloned.1.call-done = f32[1,512,2048]{2,1,0:T(8,128)} async-done(((f32[1,2048,2048]{2,1,0:T(8,128)}), f32[1,512,2048]{2,1,0:T(8,128)}) %reduce-scatter.16.cloned.1.call-update) | async-done | bytes 4194320 | tf_op jit(solution)/shard_map/reduce_scatter | solution.py:119
  1443.0 46.8 %collective-permute-done.9 = bf16[1,512,2048]{2,1,0:T(8,128)(2,1)S(1)} collective-permute-done((bf16[1,512,2048]{2,1,0:T(8,128)(2,1)}, bf16[1,512,2048]{2,1,0:T(8,128)(2,1)S(1)}, u32[]{:S(2)}, u32[]{:S(2)}) %collective-permute-start.9) | collective-permute-done | bytes 2097184 | tf_op jit(solution)/shard_map/ppermute | solution.py:103
  1489.8 43.3 %collective-permute-start.10 = (bf16[1,512,2048]{2,1,0:T(8,128)(2,1)S(1)}, bf16[1,512,2048]{2,1,0:T(8,128)(2,1)}, u32[]{:S(2)}, u32[]{:S(2)}) collective-permute-start(bf16[1,512,2048]{2,1,0:T(8,128)(2,1)S(1)} %collective-permute-done.9), channel_id=1, source_target_pairs={{0,1},{1,2},{2,3},{3,0},{4,5},{5,6},{6,7},{7,4},{8,9},{9,10},{10,1... | collective-permute-start | bytes 6291464 | tf_op jit(solution)/shard_map/ppermute | solution.py:103
  1579.8 28.2 fusion.57
  1613.9 510.6 %while.31 = (s32[]{:T(128)}, f32[4,512,2,4,64]{1,0,4,3,2:T(4,128)}, f32[4,2048,2,64]{1,3,2,0:T(8,128)}, f32[4,2048,2,64]{1,3,2,0:T(8,128)}, s32[4]{0:T(128)S(1)}...) while((s32[]{:T(128)}, f32[4,512,2,4,64]{1,0,4,3,2:T(4,128)}, ...), condition=%wide.region_14.16_spmd, body=%wide.region_12.15_spmd.sunk | while | flops 5498204672 | bytes 367659456 | solution.py:198
  1677.1 27.8 fusion.204
  1931.5 27.8 fusion.204
  2058.7 27.8 fusion.204
  2252.6 43.2 %reduce-scatter.20.cloned.1.call-done = bf16[256,512]{1,0:T(8,128)(2,1)} async-done(((bf16[2048,512]{1,0:T(8,128)(2,1)}), bf16[256,512]{1,0:T(8,128)(2,1)}) %reduce-scatter.20.cloned.1.call-update) | async-done | bytes 262160 | tf_op jit(solution)/shard_map/reduce_scatter | solution.py:334
  2297.5 280.9 %reduce-scatter.18.cloned.1.call-done = f32[1,512,2048]{2,1,0:T(8,128)} async-done(((f32[1,2048,2048]{2,1,0:T(8,128)}), f32[1,512,2048]{2,1,0:T(8,128)}) %reduce-scatter.18.cloned.1.call-update) | async-done | bytes 4194320 | tf_op jit(solution)/shard_map/reduce_scatter | solution.py:119
  2581.9 46.0 %all-reduce = (f32[2048]{0:T(1024)}, f32[2048]{0:T(1024)}) all-reduce(f32[2048]{0:T(1024)S(1)} %get-tuple-element.262, f32[2048]{0:T(1024)S(1)} %copy-done.41), channel_id=1, replica_groups=mesh['dp'=8,'tensor'=4] {'dp','tensor'}, use_global_device_ids=true, to_apply=%region_20.22 | all-reduce | flops 4096 | bytes 32768 | tf_op jit(solution)/shard_map/psum | solution.py:332
  2627.9 234.7 %reduce-scatter.14.cloned.1.call-done = f32[1,512,2048]{2,1,0:T(8,128)} async-done(((f32[1,2048,2048]{2,1,0:T(8,128)}), f32[1,512,2048]{2,1,0:T(8,128)}) %reduce-scatter.14.cloned.1.call-update) | async-done | bytes 4194320 | tf_op jit(solution)/shard_map/reduce_scatter | solution.py:119
  (316 shorter events, 1060.2 us)
Async XLA Ops:
  7.9 391.9 %all-gather.8.cloned.1.call-start = ((), (), s32[]{:S(2)}) async-start(), calls=%async_computation.12 | async-start | bytes 2359296 | tf_op jit(solution)/shard_map/all_gather | solution.py:234
  15.3 92.4 %collective-permute-start.2 = (bf16[1,512,2048]{2,1,0:T(8,128)(2,1)S(1)}, bf16[1,512,2048]{2,1,0:T(8,128)(2,1)}, u32[]{:S(2)}, u32[]{:S(2)}) collective-permute-start(bf16[1,512,2048]{2,1,0:T(8,128)(2,1)S(1)} %fusion.98), channel_id=1, source_target_pairs={{0,3},{1,0},{2,1},{3,2},{4,7},{5,4},{6,5},{7,6},{8,11},{9,8},{10,9... | collective-permute-start | bytes 6291464 | tf_op jit(solution)/shard_map/ppermute | solution.py:107
  63.9 89.0 %collective-permute-start.1 = (bf16[1,512,2048]{2,1,0:T(8,128)(2,1)}, bf16[1,512,2048]{2,1,0:T(8,128)(2,1)}, u32[]{:S(2)}, u32[]{:S(2)}) collective-permute-start(bf16[1,512,2048]{2,1,0:T(8,128)(2,1)} %collective-permute-done), channel_id=1, source_target_pairs={{0,1},{1,2},{2,3},{3,0},{4,5},{5,6},{6,7},{7,4},{8,9},{9,10},{10,1... | collective-permute-start | bytes 6291464 | tf_op jit(solution)/shard_map/ppermute | solution.py:103
  64.0 667.7 %reduce-scatter.12.cloned.1.call-start = ((), (), s32[]{:S(2)}) async-start(), calls=%async_computation.13 | async-start | bytes 20971520 | tf_op jit(solution)/shard_map/reduce_scatter | solution.py:119
  412.5 604.4 %all-gather.12.cloned.1.call-start = ((), (), s32[]{:S(2)}) async-start(), calls=%async_computation.15 | async-start | bytes 9437184 | tf_op jit(solution)/shard_map/all_gather | solution.py:266
  413.0 628.1 %all-gather.10.cloned.1.call-start = ((), (), s32[]{:S(2)}) async-start(), calls=%async_computation.14 | async-start | bytes 9437184 | tf_op jit(solution)/shard_map/all_gather | solution.py:265
  413.6 651.7 %all-gather.14.cloned.1.call-start = ((), (), s32[]{:S(2)}) async-start(), calls=%async_computation.16 | async-start | bytes 9437184 | tf_op jit(solution)/shard_map/all_gather | solution.py:267
  413.7 327.3 %collective-permute-start.6 = (bf16[1,512,2048]{2,1,0:T(8,128)(2,1)}, bf16[1,512,2048]{2,1,0:T(8,128)(2,1)}, u32[]{:S(2)}, u32[]{:S(2)}) collective-permute-start(bf16[1,512,2048]{2,1,0:T(8,128)(2,1)} %param.29), channel_id=1, source_target_pairs={{0,1},{1,2},{2,3},{3,0},{4,5},{5,6},{6,7},{7,4},{8,9},{9,10},{10,1... | collective-permute-start | bytes 6291464 | tf_op jit(solution)/shard_map/ppermute | solution.py:103
  414.2 1016.2 %reduce-scatter.16.cloned.1.call-start = ((), (), s32[]{:S(2)}) async-start(), calls=%async_computation.18 | async-start | bytes 20971520 | tf_op jit(solution)/shard_map/reduce_scatter | solution.py:119
  737.8 94.5 %collective-permute-start.8 = (bf16[1,512,2048]{2,1,0:T(8,128)(2,1)S(1)}, bf16[1,512,2048]{2,1,0:T(8,128)(2,1)S(1)}, u32[]{:S(2)}, u32[]{:S(2)}) collective-permute-start(bf16[1,512,2048]{2,1,0:T(8,128)(2,1)S(1)} %copy-done.11), channel_id=1, source_target_pairs={{0,3},{1,0},{2,1},{3,2},{4,7},{5,4},{6,5},{7,6},{8,11},{9,8},{10,9... | collective-permute-start | bytes 6291464 | tf_op jit(solution)/shard_map/ppermute | solution.py:107
  741.0 136.4 %collective-permute-start.7 = (bf16[1,512,2048]{2,1,0:T(8,128)(2,1)}, bf16[1,512,2048]{2,1,0:T(8,128)(2,1)S(1)}, u32[]{:S(2)}, u32[]{:S(2)}) collective-permute-start(bf16[1,512,2048]{2,1,0:T(8,128)(2,1)} %collective-permute-done.6), channel_id=1, source_target_pairs={{0,1},{1,2},{2,3},{3,0},{4,5},{5,6},{6,7},{7,4},{8,9},{9,10},{10,1... | collective-permute-start | bytes 6291464 | tf_op jit(solution)/shard_map/ppermute | solution.py:103
  741.0 180.7 %collective-permute-start.5 = (bf16[1,512,2048]{2,1,0:T(8,128)(2,1)S(1)}, bf16[1,512,2048]{2,1,0:T(8,128)(2,1)S(1)}, u32[]{:S(2)}, u32[]{:S(2)}) collective-permute-start(bf16[1,512,2048]{2,1,0:T(8,128)(2,1)S(1)} %multiply_convert_fusion.3), channel_id=1, source_target_pairs={{0,3},{1,0},{2,1},{3,2},{4,7},{5,4},{6,5},{7,6},{8,11},{9,8},{10,9... | collective-permute-start | bytes 6291464 | tf_op jit(solution)/shard_map/ppermute | solution.py:107
  787.5 179.0 %collective-permute-start.4 = (bf16[1,512,2048]{2,1,0:T(8,128)(2,1)S(1)}, bf16[1,512,2048]{2,1,0:T(8,128)(2,1)S(1)}, u32[]{:S(2)}, u32[]{:S(2)}) collective-permute-start(bf16[1,512,2048]{2,1,0:T(8,128)(2,1)S(1)} %collective-permute-done.3), channel_id=1, source_target_pairs={{0,1},{1,2},{2,3},{3,0},{4,5},{5,6},{6,7},{7,4},{8,9},{9,10},{10,1... | collective-permute-start | bytes 6291464 | tf_op jit(solution)/shard_map/ppermute | solution.py:103
  1150.9 1082.1 %reduce-scatter.32.cloned.1.call-start = ((), (), s32[]{:S(2)}) async-start(), calls=%async_computation.26 | async-start | bytes 9437184 | tf_op jit(solution)/shard_map/reduce_scatter | solution.py:352
  1174.7 1061.2 %reduce-scatter.30.cloned.1.call-start = ((), (), s32[]{:S(2)}) async-start(), calls=%async_computation.25 | async-start | bytes 9437184 | tf_op jit(solution)/shard_map/reduce_scatter | solution.py:349
  1199.1 1039.7 %reduce-scatter.28.cloned.1.call-start = ((), (), s32[]{:S(2)}) async-start(), calls=%async_computation.24 | async-start | bytes 9437184 | tf_op jit(solution)/shard_map/reduce_scatter | solution.py:346
  1439.2 118.4 %collective-permute-start.11 = (bf16[1,512,2048]{2,1,0:T(8,128)(2,1)}, bf16[1,512,2048]{2,1,0:T(8,128)(2,1)}, u32[]{:S(2)}, u32[]{:S(2)}) collective-permute-start(bf16[1,512,2048]{2,1,0:T(8,128)(2,1)} %fusion.126), channel_id=1, source_target_pairs={{0,3},{1,0},{2,1},{3,2},{4,7},{5,4},{6,5},{7,6},{8,11},{9,8},{10,9... | collective-permute-start | bytes 6291464 | tf_op jit(solution)/shard_map/ppermute | solution.py:107
  1489.8 90.0 %collective-permute-start.10 = (bf16[1,512,2048]{2,1,0:T(8,128)(2,1)S(1)}, bf16[1,512,2048]{2,1,0:T(8,128)(2,1)}, u32[]{:S(2)}, u32[]{:S(2)}) collective-permute-start(bf16[1,512,2048]{2,1,0:T(8,128)(2,1)S(1)} %collective-permute-done.9), channel_id=1, source_target_pairs={{0,1},{1,2},{2,3},{3,0},{4,5},{5,6},{6,7},{7,4},{8,9},{9,10},{10,1... | collective-permute-start | bytes 6291464 | tf_op jit(solution)/shard_map/ppermute | solution.py:103
  1557.5 684.1 %reduce-scatter.22.cloned.1.call-start = ((), (), s32[]{:S(2)}) async-start(), calls=%async_computation.21 | async-start | bytes 589824 | tf_op jit(solution)/shard_map/reduce_scatter | solution.py:337
  2134.0 109.1 %reduce-scatter.24.cloned.1.call-start = ((), (), s32[]{:S(2)}) async-start(), calls=%async_computation.22 | async-start | bytes 589824 | tf_op jit(solution)/shard_map/reduce_scatter | solution.py:340
  2143.3 107.5 %reduce-scatter.26.cloned.1.call-start = ((), (), s32[]{:S(2)}) async-start(), calls=%async_computation.23 | async-start | bytes 2359296 | tf_op jit(solution)/shard_map/reduce_scatter | solution.py:343
  2153.3 142.4 %reduce-scatter.20.cloned.1.call-start = ((), (), s32[]{:S(2)}) async-start(), calls=%async_computation.20 | async-start | bytes 2359296 | tf_op jit(solution)/shard_map/reduce_scatter | solution.py:334
  2173.6 404.8 %reduce-scatter.18.cloned.1.call-start = ((), (), s32[]{:S(2)}) async-start(), calls=%async_computation.19 | async-start | bytes 20971520 | tf_op jit(solution)/shard_map/reduce_scatter | solution.py:119
  2208.2 654.4 %reduce-scatter.14.cloned.1.call-start = ((), (), s32[]{:S(2)}) async-start(), calls=%async_computation.17 | async-start | bytes 20971520 | tf_op jit(solution)/shard_map/reduce_scatter | solution.py:119
  (58 other events, 6869.3 us)
Sparse Core Ops, SparseCore 0:
  9.9 30.5 all-gather.5
  64.1 70.9 all-gather.7
  412.6 319.1 reduce-scatter.11
  733.6 54.9 all-gather.11
  790.6 54.3 all-gather.9
  846.9 54.3 all-gather.13
  1151.0 279.2 reduce-scatter.15
  1433.8 71.9 reduce-scatter.31
  1509.7 71.2 reduce-scatter.29
  1584.3 71.2 reduce-scatter.27
  2134.1 33.4 reduce-scatter.21
  2171.1 34.1 reduce-scatter.23
  2209.5 41.2 reduce-scatter.25
  2254.5 41.2 reduce-scatter.19
  2298.1 280.2 reduce-scatter.17
  2580.6 281.9 reduce-scatter.13
